TPU v7x, 32 devices: a whole 2x2x4 slice. The times are simulated.
32 devices in a mesh: pts: 8 (over y, x, core), lst: 4 (over z).
Axes of the slice: x: 2, y: 2, z: 4, core: 2. Of those that a mesh axis runs over, the one named last changes fastest.
Arguments:
- tower_out: bfloat16 [16384, 1024], P('pts', 'lst'), may hold values from -6 to 6
- projection: bfloat16 [1024, 256], P('lst'), may hold values from -1 to 1
- centroids: bfloat16 [16384, 256], P('lst'), may hold values from -6 to 6
Outputs:
- new_centroids: float32 [16384, 256], P(('lst', 'pts'))
- row_log: float32 [16384], P('pts')
All inputs are finite; a program needn't handle non-finite values.
Results may differ from a plain program's by a relative error of at most 0.0045.
Values may be sent and summed in bfloat16 or wider, within the bound.
A program may use at most 64 MiB of HBM per device.

v0:
```python
import jax
import jax.numpy as jnp
from jax import lax
from jax.sharding import PartitionSpec as P

DP = 256
ITERS = 3


temper = 0.05


def rms_norm(values):
    return values * lax.rsqrt(jnp.mean(values * values, axis=-1, keepdims=True) + 1e-06)


def energy(zblock, unit_lists):
    scores = lax.dot_general(
        zblock, unit_lists, (((1,), (1,)), ((), ())), preferred_element_type=jnp.float32
    )
    return jnp.exp(scores / (DP * temper) - 1.0 / temper)


def update_terms(energy_blk, scale_blk, col_scale, zblock):
    weights = (scale_blk[:, None] * energy_blk * col_scale[None, :]).astype(jnp.bfloat16)
    return lax.dot_general(
        weights, zblock, (((0,), (0,)), ((), ())), preferred_element_type=jnp.float32
    )


def column_total(local_sum):
    return lax.psum(local_sum, "pts")


def on_device(tower_out, projection, centroids):
    point_rows = tower_out.shape[0]
    list_count = centroids.shape[0]
    total_points = point_rows * lax.axis_size("pts")
    total_lists = list_count * lax.axis_size("lst")
    balance = total_points / total_lists
    full_rows = lax.all_to_all(tower_out, "lst", split_axis=0, concat_axis=1, tiled=True)
    own_rows = jnp.dot(
        full_rows,
        lax.all_gather(projection, "lst", axis=0, tiled=True),
        preferred_element_type=jnp.float32,
    )
    normed = lax.all_gather(rms_norm(own_rows).astype(jnp.bfloat16), "lst", axis=0, tiled=True)
    unit_lists = rms_norm(centroids.astype(jnp.float32)).astype(jnp.bfloat16)
    block_rows = min(512, point_rows)
    block_count = point_rows // block_rows
    blocks = normed.reshape(block_count, block_rows, DP)
    start_sums = jnp.zeros((list_count, DP), jnp.float32)
    row_scale = jnp.ones((point_rows,), jnp.float32)
    col_scale = jnp.ones((list_count,), jnp.float32)
    for sweep in range(ITERS):

        def column_step(running, inputs):
            zblock, scale_blk = inputs
            return (
                running + jnp.sum(energy(zblock, unit_lists) * scale_blk[:, None], axis=0),
                None,
            )

        column_sum = column_total(
            lax.scan(
                column_step,
                jnp.zeros((list_count,), jnp.float32),
                (blocks, row_scale.reshape(block_count, block_rows)),
            )[0]
        )
        col_scale = balance / column_sum

        def row_step(zblock, scales=col_scale):
            return jnp.sum(energy(zblock, unit_lists) * scales[None, :], axis=1)

        row_local = lax.map(row_step, blocks).reshape(point_rows)
        row_scale = 1.0 / lax.psum(row_local, "lst")

    def update_step(running, inputs):
        zblock, scale_blk = inputs
        return (
            running + update_terms(energy(zblock, unit_lists), scale_blk, col_scale, zblock),
            None,
        )

    list_sums = lax.scan(
        update_step, start_sums, (blocks, row_scale.reshape(block_count, block_rows))
    )[0]
    owned_sums = lax.psum_scatter(list_sums, "pts", scatter_dimension=0, tiled=True)
    return (rms_norm(owned_sums), jnp.log(row_scale))


def solution(mesh):
    return jax.shard_map(
        on_device,
        mesh=mesh,
        in_specs=(P("pts", "lst"), P("lst", None), P("lst", None)),
        out_specs=(P(("lst", "pts"), None), P("pts")),
        check_vma=False,
    )
```

profile of v0, /device:TPU:0, one launch (start us, length us, event | category | flops | bytes accessed | tf_op | source)
XLA Modules:
  0.0 361.7 jit_solution(5650307541410187121)
XLA Ops:
  7.2 6.5 %all-to-all-start = ((bf16[4,512,256]{2,1,0:T(8,128)(2,1)}), bf16[4,512,256]{2,1,0:T(8,128)(2,1)S(1)}, u32[]{:S(2)}, u32[]{:S(2)}) async-start(bf16[4,512,256]{2,1,0:T(8,128)(2,1)} %bitcast.90), calls=%async_computation | async-start | bytes 2097152 | tf_op jit(solution)/shard_map/all_to_all | solution.py:41
  13.7 36.6 %all_gather.6 = bf16[1024,256]{1,0:T(8,128)(2,1)} all-gather(bf16[256,256]{1,0:T(8,128)(2,1)} %param.18), channel_id=1, replica_groups=mesh['pts'=8,'lst'=4] {'lst'}, dimensions={0}, use_global_device_ids=true | all-gather | bytes 655360 | tf_op jit(solution)/shard_map/all_gather | solution.py:44
  56.7 26.8 %all-gather.2.cloned.1.call-done = bf16[2048,256]{0,1:T(8,128)(2,1)} async-done(((bf16[512,256]{0,1:T(8,128)(2,1)}), bf16[2048,256]{0,1:T(8,128)(2,1)}) %all-gather.2.cloned.1.call-update) | async-done | bytes 1048592 | tf_op jit(solution)/shard_map/all_gather | solution.py:47
  85.0 13.7 %while.91 = (s32[]{:T(128)}, f32[4096]{0:T(1024)S(1)}, bf16[4,512,256]{2,1,0:T(8,128)(2,1)S(1)}, bf16[4096,256]{1,0:T(8,128)(2,1)}, s32[]{:T(128)}, /*index=5*/s32[]{:T(128)}) while((s32[]{:T(128)}, f32[4096]{0:T(1024)S(1)}, bf16[4,512,256]{2,1,0:T(8,128)(2,1)S(1)}, bf16[4096,256]{1,0:T(8,128)(2,1)}, s32[]{:T(128)}, ...), condition=%wide.region_4.5_spmd.clone, body=%wide.region_2.4_spmd.clone.sunk | while | flops 1080037376 | bytes 2424915 | solution.py:65
  98.7 23.5 %psum.42 = f32[4096]{0:T(1024)S(1)} all-reduce(f32[4096]{0:T(1024)S(1)} %get-tuple-element.457), channel_id=1, replica_groups=mesh['pts'=8,'lst'=4] {'pts'}, use_global_device_ids=true, to_apply=%region_5.6 | all-reduce | flops 4096 | bytes 32768 | tf_op jit(solution)/shard_map/psum | solution.py:32
  122.2 15.0 %while.88 = (s32[]{:T(128)}, f32[4,512]{1,0:T(4,128)S(1)}, bf16[4,512,256]{2,1,0:T(8,128)(2,1)S(1)}, bf16[4096,256]{1,0:T(8,128)(2,1)}, f32[4096]{0:T(1024)S(1)}, /*index=5*/s32[]{:T(128)}, s32[]{:T(128)}) while((s32[]{:T(128)}, f32[4,512]{1,0:T(4,128)S(1)}, bf16[4,512,256]{2,1,0:T(8,128)(2,1)S(1)}, bf16[4096,256]{1,0:T(8,128)(2,1)}, ...), condition=%wide.region_8.9_spmd, body=%wide.region_6.8_spmd.sunk | while | flops 1082129920 | bytes 2381909 | solution.py:76
  137.3 10.9 %psum.43 = f32[2048]{0:T(1024)S(1)} all-reduce(f32[2048]{0:T(1024)S(1)} %bitcast.102), channel_id=1, replica_groups=mesh['pts'=8,'lst'=4] {'lst'}, use_global_device_ids=true, to_apply=%region_9.10 | all-reduce | flops 2048 | bytes 16384 | tf_op jit(solution)/shard_map/psum | solution.py:77
  148.2 14.9 %while.92 = (s32[]{:T(128)}, f32[4096]{0:T(1024)S(1)}, bf16[4,512,256]{2,1,0:T(8,128)(2,1)S(1)}, bf16[4096,256]{1,0:T(8,128)(2,1)}, f32[4,512]{1,0:T(4,128)S(1)}, /*index=5*/s32[]{:T(128)}, s32[]{:T(128)}) while((s32[]{:T(128)}, f32[4096]{0:T(1024)S(1)}, bf16[4,512,256]{2,1,0:T(8,128)(2,1)S(1)}, bf16[4096,256]{1,0:T(8,128)(2,1)}, ...), condition=%wide.region_12.13_spmd.clone, body=%wide.region_10.12_spmd.clone.sunk | while | flops 1082134528 | bytes 2431071 | solution.py:65
  163.1 22.3 %psum.44 = f32[4096]{0:T(1024)S(1)} all-reduce(f32[4096]{0:T(1024)S(1)} %get-tuple-element.459), channel_id=1, replica_groups=mesh['pts'=8,'lst'=4] {'pts'}, use_global_device_ids=true, to_apply=%region_13.14 | all-reduce | flops 4096 | bytes 32768 | tf_op jit(solution)/shard_map/psum | solution.py:32
  185.4 15.0 %while.89 = (s32[]{:T(128)}, f32[4,512]{1,0:T(4,128)S(1)}, bf16[4,512,256]{2,1,0:T(8,128)(2,1)S(1)}, bf16[4096,256]{1,0:T(8,128)(2,1)}, f32[4096]{0:T(1024)S(1)}, /*index=5*/s32[]{:T(128)}, s32[]{:T(128)}) while((s32[]{:T(128)}, f32[4,512]{1,0:T(4,128)S(1)}, bf16[4,512,256]{2,1,0:T(8,128)(2,1)S(1)}, bf16[4096,256]{1,0:T(8,128)(2,1)}, ...), condition=%wide.region_16.17_spmd, body=%wide.region_14.16_spmd.sunk | while | flops 1082129920 | bytes 2381909 | solution.py:76
  200.4 8.7 %psum.45 = f32[2048]{0:T(1024)S(1)} all-reduce(f32[2048]{0:T(1024)S(1)} %bitcast.103), channel_id=1, replica_groups=mesh['pts'=8,'lst'=4] {'lst'}, use_global_device_ids=true, to_apply=%region_17.18 | all-reduce | flops 2048 | bytes 16384 | tf_op jit(solution)/shard_map/psum | solution.py:77
  209.2 14.9 %while.93 = (s32[]{:T(128)}, f32[4096]{0:T(1024)S(1)}, bf16[4,512,256]{2,1,0:T(8,128)(2,1)S(1)}, bf16[4096,256]{1,0:T(8,128)(2,1)}, f32[4,512]{1,0:T(4,128)S(1)}, /*index=5*/s32[]{:T(128)}, s32[]{:T(128)}) while((s32[]{:T(128)}, f32[4096]{0:T(1024)S(1)}, bf16[4,512,256]{2,1,0:T(8,128)(2,1)S(1)}, bf16[4096,256]{1,0:T(8,128)(2,1)}, ...), condition=%wide.region_20.21_spmd.clone, body=%wide.region_18.20_spmd.clone.sunk | while | flops 1082134528 | bytes 2431071 | solution.py:65
  224.0 22.3 %psum.46 = f32[4096]{0:T(1024)S(1)} all-reduce(f32[4096]{0:T(1024)S(1)} %get-tuple-element.461), channel_id=1, replica_groups=mesh['pts'=8,'lst'=4] {'pts'}, use_global_device_ids=true, to_apply=%region_21.22 | all-reduce | flops 4096 | bytes 32768 | tf_op jit(solution)/shard_map/psum | solution.py:32
  246.4 15.1 %while.90 = (s32[]{:T(128)}, f32[4,512]{1,0:T(4,128)S(1)}, bf16[4,512,256]{2,1,0:T(8,128)(2,1)S(1)}, bf16[4096,256]{1,0:T(8,128)(2,1)}, f32[4096]{0:T(1024)S(1)}, /*index=5*/s32[]{:T(128)}, s32[]{:T(128)}) while((s32[]{:T(128)}, f32[4,512]{1,0:T(4,128)S(1)}, bf16[4,512,256]{2,1,0:T(8,128)(2,1)S(1)}, bf16[4096,256]{1,0:T(8,128)(2,1)}, ...), condition=%wide.region_24.25_spmd, body=%wide.region_22.24_spmd.sunk | while | flops 1082129920 | bytes 2381909 | solution.py:76
  246.4 3.7 %multiply_reduce_fusion.14 = f32[512]{0:T(512)S(1)} fusion(bf16[4096,256]{1,0:T(8,128)(2,1)} %get-tuple-element.1051, f32[4096]{0:T(1024)S(1)} %get-tuple-element.1052, bf16[4,512,256]{2,1,0:T(8,128)(2,1)S(1)} %get-tuple-element.1050, s32[]{:T(128)} %get-tuple-element.1041), kind=kOutput, calls=%fused_computation.8.clone.1 | convolution fusion | flops 1082129920 | bytes 2377732 | tf_op jit(solution)/shard_map/while/body/eval_jaxpr/dot_general | solution.py:18
  250.2 3.7 %multiply_reduce_fusion.14 = f32[512]{0:T(512)S(1)} fusion(bf16[4096,256]{1,0:T(8,128)(2,1)} %get-tuple-element.1051, f32[4096]{0:T(1024)S(1)} %get-tuple-element.1052, bf16[4,512,256]{2,1,0:T(8,128)(2,1)S(1)} %get-tuple-element.1050, s32[]{:T(128)} %get-tuple-element.1041), kind=kOutput, calls=%fused_computation.8.clone.1 | convolution fusion | flops 1082129920 | bytes 2377732 | tf_op jit(solution)/shard_map/while/body/eval_jaxpr/dot_general | solution.py:18
  253.9 3.7 %multiply_reduce_fusion.14 = f32[512]{0:T(512)S(1)} fusion(bf16[4096,256]{1,0:T(8,128)(2,1)} %get-tuple-element.1051, f32[4096]{0:T(1024)S(1)} %get-tuple-element.1052, bf16[4,512,256]{2,1,0:T(8,128)(2,1)S(1)} %get-tuple-element.1050, s32[]{:T(128)} %get-tuple-element.1041), kind=kOutput, calls=%fused_computation.8.clone.1 | convolution fusion | flops 1082129920 | bytes 2377732 | tf_op jit(solution)/shard_map/while/body/eval_jaxpr/dot_general | solution.py:18
  261.5 10.5 %psum.47 = f32[2048]{0:T(1024)S(1)} all-reduce(f32[2048]{0:T(1024)S(1)} %bitcast.104), channel_id=1, replica_groups=mesh['pts'=8,'lst'=4] {'lst'}, use_global_device_ids=true, to_apply=%region_25.26 | all-reduce | flops 2048 | bytes 16384 | tf_op jit(solution)/shard_map/psum | solution.py:77
  272.7 31.3 %while.94 = (s32[]{:T(128)}, f32[4096,256]{1,0:T(8,128)}, f32[4,512]{1,0:T(4,128)S(1)}, bf16[4,512,256]{2,1,0:T(8,128)(2,1)S(1)}, bf16[4096,256]{1,0:T(8,128)(2,1)}, /*index=5*/f32[4096]{0:T(1024)S(1)}, s32[]{:T(128)}, s32[]{:T(128)}) while((s32[]{:T(128)}, f32[4096,256]{1,0:T(8,128)}, f32[4,512]{1,0:T(4,128)S(1)}, ...), condition=%wide.region_27.28_spmd.clone, body=%wide.region_26.27_spmd.clone.sunk | while | flops 2160066560 | bytes 11033699 | solution.py:86
  272.7 6.9 %convolution_add_fusion.2 = f32[4096,256]{1,0:T(8,128)} fusion(f32[4096,256]{1,0:T(8,128)} %get-tuple-element.1064, pred[]{:T(512)S(6)} %compare.15, bf16[4096,256]{1,0:T(8,128)(2,1)} %get-tuple-element.1075, f32[4096]{0:T(1024)S(1)} %get-tuple-element.1076, f32[512]{0:T(512)S(1)} %bitcast.93, bf16[4,512,256]{2,1,0:T(8,128)(2,1)S(1)} %get-tuple-element.1074, ...), kind=kOutput, calls=%fused_computation.30.clone.1 | convolution fusion | flops 2160066560 | bytes 11029505 | tf_op jit(solution)/shard_map/while/body/eval_jaxpr/dot_general | solution.py:26
  279.6 8.1 %convolution_add_fusion.2 = f32[4096,256]{1,0:T(8,128)} fusion(f32[4096,256]{1,0:T(8,128)} %get-tuple-element.1064, pred[]{:T(512)S(6)} %compare.15, bf16[4096,256]{1,0:T(8,128)(2,1)} %get-tuple-element.1075, f32[4096]{0:T(1024)S(1)} %get-tuple-element.1076, f32[512]{0:T(512)S(1)} %bitcast.93, bf16[4,512,256]{2,1,0:T(8,128)(2,1)S(1)} %get-tuple-element.1074, ...), kind=kOutput, calls=%fused_computation.30.clone.1 | convolution fusion | flops 2160066560 | bytes 11029505 | tf_op jit(solution)/shard_map/while/body/eval_jaxpr/dot_general | solution.py:26
  287.7 8.1 %convolution_add_fusion.2 = f32[4096,256]{1,0:T(8,128)} fusion(f32[4096,256]{1,0:T(8,128)} %get-tuple-element.1064, pred[]{:T(512)S(6)} %compare.15, bf16[4096,256]{1,0:T(8,128)(2,1)} %get-tuple-element.1075, f32[4096]{0:T(1024)S(1)} %get-tuple-element.1076, f32[512]{0:T(512)S(1)} %bitcast.93, bf16[4,512,256]{2,1,0:T(8,128)(2,1)S(1)} %get-tuple-element.1074, ...), kind=kOutput, calls=%fused_computation.30.clone.1 | convolution fusion | flops 2160066560 | bytes 11029505 | tf_op jit(solution)/shard_map/while/body/eval_jaxpr/dot_general | solution.py:26
  295.8 8.1 %convolution_add_fusion.2 = f32[4096,256]{1,0:T(8,128)} fusion(f32[4096,256]{1,0:T(8,128)} %get-tuple-element.1064, pred[]{:T(512)S(6)} %compare.15, bf16[4096,256]{1,0:T(8,128)(2,1)} %get-tuple-element.1075, f32[4096]{0:T(1024)S(1)} %get-tuple-element.1076, f32[512]{0:T(512)S(1)} %bitcast.93, bf16[4,512,256]{2,1,0:T(8,128)(2,1)S(1)} %get-tuple-element.1074, ...), kind=kOutput, calls=%fused_computation.30.clone.1 | convolution fusion | flops 2160066560 | bytes 11029505 | tf_op jit(solution)/shard_map/while/body/eval_jaxpr/dot_general | solution.py:26
  304.0 47.7 %reduce-scatter.2.cloned.1.call-done = f32[512,256]{1,0:T(8,128)} async-done(((f32[4096,256]{1,0:T(8,128)}), f32[512,256]{1,0:T(8,128)}) %reduce-scatter.2.cloned.1.call-update) | async-done | bytes 524304 | tf_op jit(solution)/shard_map/reduce_scatter | solution.py:89
  (94 shorter events, 88.5 us)
Async XLA Ops:
  7.2 47.2 %copy-start = (bf16[4096,256]{1,0:T(8,128)(2,1)S(1)}, bf16[4096,256]{1,0:T(8,128)(2,1)}, u32[]{:S(2)}) copy-start(bf16[4096,256]{1,0:T(8,128)(2,1)} %param.19) | copy-start | bytes 6291460
  7.2 43.1 %all-to-all-start = ((bf16[4,512,256]{2,1,0:T(8,128)(2,1)}), bf16[4,512,256]{2,1,0:T(8,128)(2,1)S(1)}, u32[]{:S(2)}, u32[]{:S(2)}) async-start(bf16[4,512,256]{2,1,0:T(8,128)(2,1)} %bitcast.90), calls=%async_computation | async-start | bytes 2097152 | tf_op jit(solution)/shard_map/all_to_all | solution.py:41
  13.7 69.8 %all-gather.2.cloned.1.call-start = ((), (), s32[]{:S(2)}) async-start(), calls=%async_computation.2 | async-start | bytes 1310720 | tf_op jit(solution)/shard_map/all_gather | solution.py:47
  54.2 297.4 %reduce-scatter.2.cloned.1.call-start = ((), (), s32[]{:S(2)}) async-start(), calls=%async_computation.3 | async-start | bytes 4718592 | tf_op jit(solution)/shard_map/reduce_scatter | solution.py:89
Sparse Core Ops, SparseCore 0:
  54.3 29.1 all-gather.1
  304.1 47.5 reduce-scatter.1
where the time goes:
time: 363 us; the launch traced here: 362 us
  blocking collectives  135 us (37%)
  matrix products  120 us (33%)
  waiting for transfers between devices  74.5 us (21%)
  between operations  14.2 us (4%)
  other arithmetic  7 us (2%)
  starting transfers between devices  6.53 us (2%)
    dot_general x24, matrix products, energy(): lax.dot_general(zblock, unit_lists, (((1,), (1,)), ((), ())), preferred_e...  87.2 us
    psum x3, blocking collectives, column_total(): return lax.psum(local_sum, 'pts')  68.1 us
    reduce_scatter x1, waiting for transfers between devices, on_device(): lax.psum_scatter(list_sums, 'pts', scatter_dimension=0, tiled=True)  47.7 us
    all_gather x1, blocking collectives, on_device(): lax.all_gather(projection, 'lst', axis=0, tiled=True)  36.6 us
    dot_general x4, matrix products, update_terms(): lax.dot_general(weights, zblock, (((0,), (0,)), ((), ())), preferred_elem...  31.2 us
    psum x3, blocking collectives, on_device(): row_scale = 1.0 / lax.psum(row_local, 'lst')  30.1 us
    all_gather x1, waiting for transfers between devices, on_device(): lax.all_gather(rms_norm(own_rows).astype(jnp.bfloat16), 'lst', axis=0, ti...  26.8 us
  transfers between devices with their start and end apart: 3, of which 2 were waited for; matrix products, arithmetic and copies ran while one was open for 1% of the time, Pallas kernels for 0%

commit v1 on v0

v1 whole, which is shorter than its diff:
```python
import functools
import math

import jax
import jax.numpy as jnp
from jax import lax
from jax.experimental import pallas as pl
from jax.experimental.pallas import tpu as pltpu
from jax.sharding import PartitionSpec as P

ITERS = 3
temper = 0.05
LANES = 128
MESH = pl.DeviceIdType.MESH
F32 = jnp.float32
BF16 = jnp.bfloat16


def rms_norm(values):
    return values * lax.rsqrt(jnp.mean(values * values, axis=-1, keepdims=True) + 1e-06)


def column_of(row, rows):
    return jnp.broadcast_to(row, (rows, LANES)).T


def kernel(
    npts,
    nlst,
    tower,
    proj,
    cent,
    out,
    row_log,
    energy,
    unit,
    full,
    pfull,
    normed,
    lane_sums,
    col_sums,
    row_sums,
    col_wide,
    scaled,
    pair_send,
    pair_recv,
    chip_send,
    chip_recv,
    mine,
    t_send,
    t_recv,
    p_send,
    p_recv,
    n_send,
    n_recv,
    c_send,
    c_recv,
    r_send,
    r_recv,
    x_send,
    x_recv,
    y_send,
    y_recv,
):
    pts = lax.axis_index("pts")
    lst = lax.axis_index("lst")
    lists, dp = cent.shape
    points = tower.shape[0]
    share = points // nlst
    own = lists // npts
    chips = npts // 2
    core = pts % 2
    chip = pts // 2
    balance = (points * npts) / (lists * nlst)
    list_blocks = lists // LANES
    point_blocks = points // LANES

    barrier = pltpu.get_barrier_semaphore()
    for d in range(1, nlst):
        pl.semaphore_signal(
            barrier, inc=1, device_id={"lst": (lst + d) % nlst}, device_id_type=MESH
        )
    for d in range(1, npts):
        pl.semaphore_signal(
            barrier, inc=1, device_id={"pts": (pts + d) % npts}, device_id_type=MESH
        )
    pl.semaphore_wait(barrier, nlst + npts - 2)

    pending = []

    def send(src, dst, send_sem, recv_sem, axis, target):
        copy = pltpu.make_async_remote_copy(
            src_ref=src,
            dst_ref=dst,
            send_sem=send_sem,
            recv_sem=recv_sem,
            device_id={axis: target},
            device_id_type=MESH,
        )
        copy.start()
        pending.append(copy)
        return copy

    p_copies = [
        send(proj, pfull.at[d], p_send.at[d], p_recv.at[d], "lst", (lst + d) % nlst)
        for d in range(1, nlst)
    ]
    t_copies = []
    for d in range(1, nlst):
        z = (lst + d) % nlst
        t_copies.append(
            send(
                tower.at[pl.ds(pl.multiple_of(z * share, share), share)],
                full.at[d],
                t_send.at[d],
                t_recv.at[d],
                "lst",
                z,
            )
        )

    unit_rows = min(256, lists)

    @pl.loop(0, lists // unit_rows)
    def _(b):
        rows = pl.ds(pl.multiple_of(b * unit_rows, unit_rows), unit_rows)
        unit[rows, :] = rms_norm(cent[rows, :].astype(F32)).astype(BF16)
        lane_sums[rows, :] = jnp.zeros((unit_rows, LANES), F32)

    hidden = jnp.dot(
        tower[pl.ds(pl.multiple_of(lst * share, share), share), :],
        proj[...],
        preferred_element_type=F32,
    )
    for d in range(1, nlst):
        p_copies[d - 1].wait_recv()
        t_copies[d - 1].wait_recv()
        hidden += jnp.dot(full[d], pfull[d], preferred_element_type=F32)
    normed[0] = rms_norm(hidden).astype(BF16)
    n_copies = [
        send(normed.at[0], normed.at[d], n_send.at[d], n_recv.at[d], "lst", (lst + d) % nlst)
        for d in range(1, nlst)
    ]

    log2e = 1.0 / math.log(2.0)
    gain = log2e / (dp * temper)
    shift = -log2e / temper
    e_rows = min(256, lists)
    for d in range(nlst):
        if d:
            n_copies[d - 1].wait_recv()

        @pl.loop(0, lists // e_rows)
        def _(b, d=d):
            rows = pl.ds(pl.multiple_of(b * e_rows, e_rows), e_rows)
            sums = lane_sums[rows, :]
            step = min(256, share)
            for k in range(share // step):
                scores = lax.dot_general(
                    unit[rows, :],
                    normed[d, k * step : (k + 1) * step, :],
                    (((1,), (1,)), ((), ())),
                    preferred_element_type=F32,
                )
                block = jnp.exp2(scores * gain + shift)
                at = d * share + k * step
                energy[rows, at : at + step] = block
                for m in range(step // LANES):
                    sums += block[:, m * LANES : (m + 1) * LANES]
            lane_sums[rows, :] = sums

    def lane_dense(sums):
        return jnp.sum(sums.T, axis=0, keepdims=True)

    row_scale = None
    for sweep in range(ITERS):

        @pl.loop(0, list_blocks)
        def _(b, sweep=sweep, row_scale=row_scale):
            rows = pl.ds(pl.multiple_of(b * LANES, LANES), LANES)
            if sweep == 0:
                sums = lane_sums[rows, :]
            else:
                sums = energy[rows, 0:LANES] * row_scale[:, 0:LANES]
                for m in range(1, point_blocks):
                    lanes = slice(m * LANES, (m + 1) * LANES)
                    sums += energy[rows, lanes] * row_scale[:, lanes]
            col_sums[sweep, 0, pl.ds(b, 1), :] = lane_dense(sums)

        copies = [
            send(
                col_sums.at[sweep, 0],
                col_sums.at[sweep, d],
                c_send.at[sweep, d],
                c_recv.at[sweep, d],
                "pts",
                (pts + d) % npts,
            )
            for d in range(1, npts)
        ]
        for copy in copies:
            copy.wait_recv()
        total = col_sums[sweep, 0]
        for d in range(1, npts):
            total += col_sums[sweep, d]
        lane_sums[0:list_blocks, :] = balance / total

        def row_step(b, acc):
            rows = pl.ds(pl.multiple_of(b * LANES, LANES), LANES)
            wide = column_of(lane_sums[pl.ds(b, 1), :], LANES)
            if sweep == ITERS - 1:
                col_wide[rows, :] = wide
            parts = []
            for m in range(point_blocks):
                lanes = slice(m * LANES, (m + 1) * LANES)
                term = energy[rows, lanes] * wide
                parts.append(acc[m] + jnp.sum(term.reshape(LANES // 8, 8, LANES), axis=0))
            return tuple(parts)

        acc = lax.fori_loop(
            0,
            list_blocks,
            row_step,
            tuple(jnp.zeros((8, LANES), F32) for _ in range(point_blocks)),
        )
        per_slot = share // LANES
        for d in range(nlst):
            z = (lst + nlst - d) % nlst
            parts = [
                jnp.sum(acc[d * per_slot + m], axis=0, keepdims=True) for m in range(per_slot)
            ]
            row_sums[sweep, 0, pl.ds(z, 1), :] = jnp.concatenate(parts, axis=1)
        copies = [
            send(
                row_sums.at[sweep, 0],
                row_sums.at[sweep, d],
                r_send.at[sweep, d],
                r_recv.at[sweep, d],
                "lst",
                (lst + d) % nlst,
            )
            for d in range(1, nlst)
        ]
        for copy in copies:
            copy.wait_recv()
        total = row_sums[sweep, 0]
        for d in range(1, nlst):
            total += row_sums[sweep, d]
        scale = 1.0 / total
        row_log[...] = scale
        row_scale = jnp.concatenate(
            [row_log[pl.ds((lst + nlst - d) % nlst, 1), :] for d in range(nlst)], axis=1
        )
    row_log[...] = jnp.log(scale)

    for m in range(point_blocks):
        d, k = divmod(m * LANES, share)
        wide = column_of(row_scale[:, m * LANES : (m + 1) * LANES], LANES)
        block = normed[d, k : k + LANES, :].astype(F32)
        for h in range(dp // LANES):
            lanes = slice(h * LANES, (h + 1) * LANES)
            scaled[m * LANES : (m + 1) * LANES, lanes] = (block[:, lanes] * wide).astype(BF16)

    tile = min(256, own)

    def partial_sums(owner, store):
        @pl.loop(0, own // tile)
        def _(t):
            rows = pl.ds(pl.multiple_of(owner * own + t * tile, tile), tile)
            store(
                pl.ds(pl.multiple_of(t * tile, tile), tile),
                jnp.dot(energy[rows, :].astype(BF16), scaled[...], preferred_element_type=F32),
            )

    partner = pts + 1 - 2 * core
    x_copies = []
    order = [d % chips for d in range(1, chips + 1)]
    for d in order:

        def to_pair(rows, values, d=d):
            pair_send[d, rows, :] = values.astype(BF16)

        partial_sums(((chip + d) % chips) * 2 + 1 - core, to_pair)
        x_copies.append(
            send(pair_send.at[d], pair_recv.at[d], x_send.at[d], x_recv.at[d], "pts", partner)
        )
    y_copies = []
    for n, d in enumerate(order):

        def to_mine(rows, values):
            mine[rows, :] = values

        owner = ((chip + d) % chips) * 2 + core
        partial_sums(owner, to_mine)
        x_copies[n].wait_recv()
        pair = mine[...] + pair_recv[d].astype(F32)
        if d:
            chip_send[d] = pair.astype(BF16)
            y_copies.append(
                send(chip_send.at[d], chip_recv.at[d], y_send.at[d], y_recv.at[d], "pts", owner)
            )
        else:
            mine[...] = pair
    for copy in y_copies:
        copy.wait_recv()
    sums = mine[...]
    for d in range(1, chips):
        sums += chip_recv[d].astype(F32)
    wide = col_wide[pl.ds(pl.multiple_of(pts * own, own), own), :]
    sums = sums * jnp.concatenate([wide] * (dp // LANES), axis=1)
    out[...] = rms_norm(sums)
    for copy in pending:
        copy.wait_send()


def on_device(npts, nlst, tower_out, projection, centroids):
    points = tower_out.shape[0]
    lists, dp = centroids.shape
    feats = tower_out.shape[1]
    share = points // nlst
    own = lists // npts
    chips = npts // 2
    vmem = pl.BlockSpec(memory_space=pltpu.VMEM)
    sem = pltpu.SemaphoreType.DMA
    centers, row_log = pl.pallas_call(
        functools.partial(kernel, npts, nlst),
        out_shape=(
            jax.ShapeDtypeStruct((own, dp), F32),
            jax.ShapeDtypeStruct((nlst, share), F32),
        ),
        in_specs=[vmem] * 3,
        out_specs=(vmem, vmem),
        scratch_shapes=[
            pltpu.VMEM((lists, points), F32),
            pltpu.VMEM((lists, dp), BF16),
            pltpu.VMEM((nlst, share, feats), BF16),
            pltpu.VMEM((nlst, feats, dp), BF16),
            pltpu.VMEM((nlst, share, dp), BF16),
            pltpu.VMEM((lists, LANES), F32),
            pltpu.VMEM((ITERS, npts, lists // LANES, LANES), F32),
            pltpu.VMEM((ITERS, nlst, nlst, share), F32),
            pltpu.VMEM((lists, LANES), F32),
            pltpu.VMEM((points, dp), BF16),
            pltpu.VMEM((chips, own, dp), BF16),
            pltpu.VMEM((chips, own, dp), BF16),
            pltpu.VMEM((chips, own, dp), BF16),
            pltpu.VMEM((chips, own, dp), BF16),
            pltpu.VMEM((own, dp), F32),
            sem((nlst,)),
            sem((nlst,)),
            sem((nlst,)),
            sem((nlst,)),
            sem((nlst,)),
            sem((nlst,)),
            sem((ITERS, npts)),
            sem((ITERS, npts)),
            sem((ITERS, nlst)),
            sem((ITERS, nlst)),
            sem((chips,)),
            sem((chips,)),
            sem((chips,)),
            sem((chips,)),
        ],
        compiler_params=pltpu.CompilerParams(
            collective_id=0, has_side_effects=True, vmem_limit_bytes=64000000
        ),
    )(tower_out, projection, centroids)
    return centers, row_log.reshape(points)


def solution(mesh):
    return jax.shard_map(
        functools.partial(on_device, mesh.shape["pts"], mesh.shape["lst"]),
        mesh=mesh,
        in_specs=(P("pts", "lst"), P("lst", None), P("lst", None)),
        out_specs=(P(("lst", "pts"), None), P("pts")),
        check_vma=False,
    )
```

time: 363 us -> 148 us (0.41)
  Pallas kernels: 0 us -> 144 us
  blocking collectives: 135 us -> 0 us
  matrix products: 120 us -> 0 us
  waiting for transfers between devices: 74.5 us -> 0 us
  between operations: 14.2 us -> 0.64 us
  other arithmetic: 7 us -> 0 us
  starting transfers between devices: 6.53 us -> 0 us
    pallas_call x0 -> x1, Pallas kernels: none -> 144 us  [on_device(): pl.pallas_call(functools.partial(kernel, npts, nlst), out_shape=(jax.Shap...]
    dot_general x29 -> x0, matrix products: 120 us -> none  [the longest x24 87.2 us: energy(): lax.dot_general(zblock, unit_lists, (((1,), (1,)), ((), ())), preferred_e...]
    psum x6 -> x0, blocking collectives: 98.2 us -> none  [the longest x3 68.1 us: column_total(): return lax.psum(local_sum, 'pts')]
    reduce_scatter x1 -> x0, waiting for transfers between devices: 47.7 us -> none  [on_device(): lax.psum_scatter(list_sums, 'pts', scatter_dimension=0, tiled=True)]
    all_gather x1 -> x0, blocking collectives: 36.6 us -> none  [on_device(): lax.all_gather(projection, 'lst', axis=0, tiled=True)]
    all_gather x1 -> x0, waiting for transfers between devices: 26.8 us -> none  [on_device(): lax.all_gather(rms_norm(own_rows).astype(jnp.bfloat16), 'lst', axis=0, ti...]
    all_to_all x1 -> x0, starting transfers between devices: 6.49 us -> none  [on_device(): lax.all_to_all(tower_out, 'lst', split_axis=0, concat_axis=1, tiled=True)]
  transfers between devices with their start and end apart: 3 -> 0, of which waited for: 2 -> 0; matrix products, arithmetic and copies ran while one was open for 1% -> 0% of each run, Pallas kernels for 0% -> 0%
where the time goes in v1:
time: 148 us
  Pallas kernels  144 us (97%)
  local copies, waits for them, and re-layouts  3.17 us (2%)
    pallas_call x1, Pallas kernels, on_device(): pl.pallas_call(functools.partial(kernel, npts, nlst), out_shape=(jax.Shap...  144 us
    unnamed x2, local copies, waits for them, and re-layouts  3.17 us

profile of v1, /device:TPU:0, one launch (start us, length us, event | category | flops | bytes accessed | tf_op | source)
XLA Modules:
  0.0 147.9 jit_solution(5772184891265715265)
XLA Ops:
  0.6 144.1 %shard_map.50 = (f32[512,256]{1,0:T(8,128)}, f32[4,512]{1,0:T(4,128)}) custom-call(bf16[2048,256]{1,0:T(8,128)(2,1)} %tower.1, bf16[256,256]{1,0:T(8,128)(2,1)} %proj.1, bf16[4096,256]{1,0:T(8,128)(2,1)} %cent.1), custom_call_target="tpu_custom_call" | custom-call | tf_op jit(solution)/shard_map/pallas_call | solution.py:325
  144.7 1.3 copy.5
  146.0 1.9 %copy.7 = f32[512,256]{1,0:T(8,128)} copy(f32[512,256]{1,0:T(8,128)} %get-tuple-element.8) | data formatting | bytes 1048576

commit v2 on v1

--- a/solution.py
+++ b/solution.py
@@ -27,6 +27,7 @@
 def kernel(
     npts,
     nlst,
+    chunks,
     tower,
     proj,
     cent,
@@ -51,6 +52,8 @@
     t_recv,
     p_send,
     p_recv,
+    q_send,
+    q_recv,
     n_send,
     n_recv,
     c_send,
@@ -101,24 +104,39 @@
         pending.append(copy)
         return copy
 
+    feats = proj.shape[0]
+    piece = feats // npts
+    sliced = piece % 16 == 0
+    if sliced:
+        piece_rows = pl.ds(pl.multiple_of(pts * piece, piece), piece)
+    else:
+        piece_rows = pl.ds(0, feats)
     p_copies = [
-        send(proj, pfull.at[d], p_send.at[d], p_recv.at[d], "lst", (lst + d) % nlst)
+        send(
+            proj.at[piece_rows],
+            pfull.at[d, piece_rows],
+            p_send.at[d],
+            p_recv.at[d],
+            "lst",
+            (lst + d) % nlst,
+        )
         for d in range(1, nlst)
     ]
+    chunk = share // chunks
     t_copies = []
-    for d in range(1, nlst):
-        z = (lst + d) % nlst
-        t_copies.append(
-            send(
-                tower.at[pl.ds(pl.multiple_of(z * share, share), share)],
-                full.at[d],
-                t_send.at[d],
-                t_recv.at[d],
-                "lst",
-                z,
-            )
-        )
-
+    for c in range(chunks):
+        for d in range(1, nlst):
+            z = (lst + d) % nlst
+            t_copies.append(
+                send(
+                    tower.at[pl.ds(pl.multiple_of(z * share + c * chunk, chunk), chunk)],
+                    full.at[c, d],
+                    t_send.at[c, d],
+                    t_recv.at[c, d],
+                    "lst",
+                    z,
+                )
+            )
     unit_rows = min(256, lists)
 
     @pl.loop(0, lists // unit_rows)
@@ -127,47 +145,113 @@
         unit[rows, :] = rms_norm(cent[rows, :].astype(F32)).astype(BF16)
         lane_sums[rows, :] = jnp.zeros((unit_rows, LANES), F32)
 
-    hidden = jnp.dot(
-        tower[pl.ds(pl.multiple_of(lst * share, share), share), :],
-        proj[...],
-        preferred_element_type=F32,
-    )
-    for d in range(1, nlst):
-        p_copies[d - 1].wait_recv()
-        t_copies[d - 1].wait_recv()
-        hidden += jnp.dot(full[d], pfull[d], preferred_element_type=F32)
-    normed[0] = rms_norm(hidden).astype(BF16)
-    n_copies = [
-        send(normed.at[0], normed.at[d], n_send.at[d], n_recv.at[d], "lst", (lst + d) % nlst)
-        for d in range(1, nlst)
-    ]
+    for copy in p_copies:
+        copy.wait_recv()
+    if sliced:
+        q_copies = [
+            send(
+                pfull.at[pl.ds(1, nlst - 1), piece_rows],
+                pfull.at[pl.ds(1, nlst - 1), piece_rows],
+                q_send.at[d],
+                q_recv.at[d],
+                "pts",
+                (pts + d) % npts,
+            )
+            for d in range(1, npts)
+        ]
+
+    if sliced:
+        for copy in q_copies:
+            copy.wait_recv()
+
+    def hop(c, origin, left):
+        side = 0 if left else 1
+        return pltpu.make_async_remote_copy(
+            src_ref=normed.at[c, origin],
+            dst_ref=normed.at[c, origin],
+            send_sem=n_send.at[side, c, origin],
+            recv_sem=n_recv.at[c, origin],
+            device_id={"lst": lst - 1 if left else lst + 1},
+            device_id_type=MESH,
+        )
+
+    has_left = lst > 0
+    has_right = lst < nlst - 1
+    for c in range(chunks):
+        hidden = jnp.dot(
+            tower[pl.ds(pl.multiple_of(lst * share + c * chunk, chunk), chunk), :],
+            proj[...],
+            preferred_element_type=F32,
+        )
+        for d in range(1, nlst):
+            t_copies[c * (nlst - 1) + d - 1].wait_recv()
+            hidden += jnp.dot(full[c, d], pfull[d], preferred_element_type=F32)
+        normed[c, lst] = rms_norm(hidden).astype(BF16)
+
+        @pl.when(has_left)
+        def _(c=c):
+            hop(c, lst, True).start()
+
+        @pl.when(has_right)
+        def _(c=c):
+            hop(c, lst, False).start()
 
     log2e = 1.0 / math.log(2.0)
     gain = log2e / (dp * temper)
     shift = -log2e / temper
     e_rows = min(256, lists)
-    for d in range(nlst):
-        if d:
-            n_copies[d - 1].wait_recv()
-
+    step = min(256, chunk)
+
+    def energy_of(c, origin):
         @pl.loop(0, lists // e_rows)
-        def _(b, d=d):
+        def _(b):
             rows = pl.ds(pl.multiple_of(b * e_rows, e_rows), e_rows)
             sums = lane_sums[rows, :]
-            step = min(256, share)
-            for k in range(share // step):
+            for k in range(chunk // step):
                 scores = lax.dot_general(
                     unit[rows, :],
-                    normed[d, k * step : (k + 1) * step, :],
+                    normed[c, origin, k * step : (k + 1) * step, :],
                     (((1,), (1,)), ((), ())),
                     preferred_element_type=F32,
                 )
                 block = jnp.exp2(scores * gain + shift)
-                at = d * share + k * step
-                energy[rows, at : at + step] = block
+                at = pl.multiple_of(origin * share + c * chunk + k * step, step)
+                energy[rows, pl.ds(at, step)] = block
                 for m in range(step // LANES):
                     sums += block[:, m * LANES : (m + 1) * LANES]
             lane_sums[rows, :] = sums
+
+    paired = jnp.minimum(lst, nlst - 1 - lst)
+    for s in range(nlst):
+        near = (s + 1) // 2
+        far = s - paired
+        in_pairs = lst - near if s % 2 else lst + near
+        beyond = jnp.where(has_right & (lst < nlst - 1 - lst), lst + far, lst - far)
+        origin = jnp.where(s <= 2 * paired, in_pairs, beyond) if s else lst
+        for c in range(chunks):
+            if s:
+                hop(c, origin, True).wait_recv()
+
+                @pl.when((origin < lst) & has_right)
+                def _(c=c, origin=origin):
+                    hop(c, origin, False).start()
+
+                @pl.when((origin > lst) & has_left)
+                def _(c=c, origin=origin):
+                    hop(c, origin, True).start()
+
+            energy_of(c, origin)
+
+    for z in range(nlst):
+        for c in range(chunks):
+
+            @pl.when((z <= lst) & has_right)
+            def _(c=c, z=z):
+                hop(c, z, False).wait_send()
+
+            @pl.when((z >= lst) & has_left)
+            def _(c=c, z=z):
+                hop(c, z, True).wait_send()
 
     def lane_dense(sums):
         return jnp.sum(sums.T, axis=0, keepdims=True)
@@ -225,11 +309,10 @@
         )
         per_slot = share // LANES
         for d in range(nlst):
-            z = (lst + nlst - d) % nlst
             parts = [
                 jnp.sum(acc[d * per_slot + m], axis=0, keepdims=True) for m in range(per_slot)
             ]
-            row_sums[sweep, 0, pl.ds(z, 1), :] = jnp.concatenate(parts, axis=1)
+            row_sums[sweep, 0, d : d + 1, :] = jnp.concatenate(parts, axis=1)
         copies = [
             send(
                 row_sums.at[sweep, 0],
@@ -247,16 +330,14 @@
         for d in range(1, nlst):
             total += row_sums[sweep, d]
         scale = 1.0 / total
-        row_log[...] = scale
-        row_scale = jnp.concatenate(
-            [row_log[pl.ds((lst + nlst - d) % nlst, 1), :] for d in range(nlst)], axis=1
-        )
+        row_scale = jnp.concatenate([scale[d : d + 1, :] for d in range(nlst)], axis=1)
     row_log[...] = jnp.log(scale)
 
     for m in range(point_blocks):
         d, k = divmod(m * LANES, share)
         wide = column_of(row_scale[:, m * LANES : (m + 1) * LANES], LANES)
-        block = normed[d, k : k + LANES, :].astype(F32)
+        c, k = divmod(k, chunk)
+        block = normed[c, d, k : k + LANES, :].astype(F32)
         for h in range(dp // LANES):
             lanes = slice(h * LANES, (h + 1) * LANES)
             scaled[m * LANES : (m + 1) * LANES, lanes] = (block[:, lanes] * wide).astype(BF16)
@@ -320,10 +401,12 @@
     share = points // nlst
     own = lists // npts
     chips = npts // 2
+    chunks = 2 if share % (2 * LANES) == 0 else 1
+    chunk = share // chunks
     vmem = pl.BlockSpec(memory_space=pltpu.VMEM)
     sem = pltpu.SemaphoreType.DMA
     centers, row_log = pl.pallas_call(
-        functools.partial(kernel, npts, nlst),
+        functools.partial(kernel, npts, nlst, chunks),
         out_shape=(
             jax.ShapeDtypeStruct((own, dp), F32),
             jax.ShapeDtypeStruct((nlst, share), F32),
@@ -333,9 +416,9 @@
         scratch_shapes=[
             pltpu.VMEM((lists, points), F32),
             pltpu.VMEM((lists, dp), BF16),
-            pltpu.VMEM((nlst, share, feats), BF16),
+            pltpu.VMEM((chunks, nlst, chunk, feats), BF16),
             pltpu.VMEM((nlst, feats, dp), BF16),
-            pltpu.VMEM((nlst, share, dp), BF16),
+            pltpu.VMEM((chunks, nlst, chunk, dp), BF16),
             pltpu.VMEM((lists, LANES), F32),
             pltpu.VMEM((ITERS, npts, lists // LANES, LANES), F32),
             pltpu.VMEM((ITERS, nlst, nlst, share), F32),
@@ -346,12 +429,14 @@
             pltpu.VMEM((chips, own, dp), BF16),
             pltpu.VMEM((chips, own, dp), BF16),
             pltpu.VMEM((own, dp), F32),
+            sem((chunks, nlst)),
+            sem((chunks, nlst)),
             sem((nlst,)),
             sem((nlst,)),
-            sem((nlst,)),
-            sem((nlst,)),
-            sem((nlst,)),
-            sem((nlst,)),
+            sem((npts,)),
+            sem((npts,)),
+            sem((2, chunks, nlst)),
+            sem((chunks, nlst)),
             sem((ITERS, npts)),
             sem((ITERS, npts)),
             sem((ITERS, nlst)),

time: 148 us -> 140 us (0.946)
  Pallas kernels: 144 us -> 136 us
    pallas_call x1, Pallas kernels: 144 us -> 136 us  [on_device(): pl.pallas_call(functools.partial(kernel, npts, nlst, chunks), out_shape=(...]
where the time goes in v2:
time: 140 us; the launch traced here: 139 us
  Pallas kernels  136 us (97%)
  local copies, waits for them, and re-layouts  3.17 us (2%)
    pallas_call x1, Pallas kernels, on_device(): pl.pallas_call(functools.partial(kernel, npts, nlst, chunks), out_shape=(...  136 us
    unnamed x2, local copies, waits for them, and re-layouts  3.17 us

profile of v2, /device:TPU:0, one launch (start us, length us, event | category | flops | bytes accessed | tf_op | source)
XLA Modules:
  0.0 139.4 jit_solution(1887088468847297293)
XLA Ops:
  0.6 135.6 %shard_map.50 = (f32[512,256]{1,0:T(8,128)}, f32[4,512]{1,0:T(4,128)}) custom-call(bf16[2048,256]{1,0:T(8,128)(2,1)} %tower.1, bf16[256,256]{1,0:T(8,128)(2,1)} %proj.1, bf16[4096,256]{1,0:T(8,128)(2,1)} %cent.1), custom_call_target="tpu_custom_call" | custom-call | tf_op jit(solution)/shard_map/pallas_call | solution.py:408
  136.2 1.3 copy.5
  137.5 1.9 %copy.7 = f32[512,256]{1,0:T(8,128)} copy(f32[512,256]{1,0:T(8,128)} %get-tuple-element.8) | data formatting | bytes 1048576

commit v3 on v2

--- a/solution.py
+++ b/solution.py
@@ -199,7 +199,7 @@
     log2e = 1.0 / math.log(2.0)
     gain = log2e / (dp * temper)
     shift = -log2e / temper
-    e_rows = min(256, lists)
+    e_rows = min(1024, lists)
     step = min(256, chunk)
 
     def energy_of(c, origin):
@@ -259,7 +259,7 @@
     row_scale = None
     for sweep in range(ITERS):
 
-        @pl.loop(0, list_blocks)
+        @pl.loop(0, list_blocks, unroll=2)
         def _(b, sweep=sweep, row_scale=row_scale):
             rows = pl.ds(pl.multiple_of(b * LANES, LANES), LANES)
             if sweep == 0:
@@ -306,6 +306,7 @@
             list_blocks,
             row_step,
             tuple(jnp.zeros((8, LANES), F32) for _ in range(point_blocks)),
+            unroll=2,
         )
         per_slot = share // LANES
         for d in range(nlst):

time: 140 us -> 117 us (0.84)
  Pallas kernels: 136 us -> 113 us
    pallas_call x1, Pallas kernels: 136 us -> 113 us  [on_device(): pl.pallas_call(functools.partial(kernel, npts, nlst, chunks), out_shape=(...]
where the time goes in v3:
time: 117 us; the launch traced here: 116 us
  Pallas kernels  113 us (97%)
  local copies, waits for them, and re-layouts  3.17 us (3%)
    pallas_call x1, Pallas kernels, on_device(): pl.pallas_call(functools.partial(kernel, npts, nlst, chunks), out_shape=(...  113 us
    unnamed x2, local copies, waits for them, and re-layouts  3.17 us

profile of v3, /device:TPU:0, one launch (start us, length us, event | category | flops | bytes accessed | tf_op | source)
XLA Modules:
  0.0 116.3 jit_solution(11925800066782392862)
XLA Ops:
  0.6 112.5 %shard_map.50 = (f32[512,256]{1,0:T(8,128)}, f32[4,512]{1,0:T(4,128)}) custom-call(bf16[2048,256]{1,0:T(8,128)(2,1)} %tower.1, bf16[256,256]{1,0:T(8,128)(2,1)} %proj.1, bf16[4096,256]{1,0:T(8,128)(2,1)} %cent.1), custom_call_target="tpu_custom_call" | custom-call | tf_op jit(solution)/shard_map/pallas_call | solution.py:409
  113.2 1.3 %copy.5 = f32[1,4,4,128]{3,1,2,0:T(4,128)} copy(f32[1,4,4,128]{3,2,1,0:T(4,128)} %bitcast.3) | data formatting | bytes 16384
  114.5 1.9 %copy.7 = f32[512,256]{1,0:T(8,128)} copy(f32[512,256]{1,0:T(8,128)} %get-tuple-element.8) | data formatting | bytes 1048576

commit v4 on v3

--- a/solution.py
+++ b/solution.py
@@ -259,7 +259,7 @@
     row_scale = None
     for sweep in range(ITERS):
 
-        @pl.loop(0, list_blocks, unroll=2)
+        @pl.loop(0, list_blocks, unroll=4)
         def _(b, sweep=sweep, row_scale=row_scale):
             rows = pl.ds(pl.multiple_of(b * LANES, LANES), LANES)
             if sweep == 0:
@@ -306,7 +306,7 @@
             list_blocks,
             row_step,
             tuple(jnp.zeros((8, LANES), F32) for _ in range(point_blocks)),
-            unroll=2,
+            unroll=4,
         )
         per_slot = share // LANES
         for d in range(nlst):

time: 117 us -> 113 us (0.966)
  Pallas kernels: 113 us -> 109 us
    pallas_call x1, Pallas kernels: 113 us -> 109 us  [on_device(): pl.pallas_call(functools.partial(kernel, npts, nlst, chunks), out_shape=(...]
where the time goes in v4:
time: 113 us
  Pallas kernels  109 us (96%)
  local copies, waits for them, and re-layouts  3.17 us (3%)
    pallas_call x1, Pallas kernels, on_device(): pl.pallas_call(functools.partial(kernel, npts, nlst, chunks), out_shape=(...  109 us
    unnamed x2, local copies, waits for them, and re-layouts  3.17 us

profile of v4, /device:TPU:0, one launch (start us, length us, event | category | flops | bytes accessed | tf_op | source)
XLA Modules:
  0.0 112.7 jit_solution(10440833279488942893)
XLA Ops:
  0.6 108.9 %shard_map.50 = (f32[512,256]{1,0:T(8,128)}, f32[4,512]{1,0:T(4,128)}) custom-call(bf16[2048,256]{1,0:T(8,128)(2,1)} %tower.1, bf16[256,256]{1,0:T(8,128)(2,1)} %proj.1, bf16[4096,256]{1,0:T(8,128)(2,1)} %cent.1), custom_call_target="tpu_custom_call" | custom-call | tf_op jit(solution)/shard_map/pallas_call | solution.py:409
  109.6 1.3 %copy.5 = f32[1,4,4,128]{3,1,2,0:T(4,128)} copy(f32[1,4,4,128]{3,2,1,0:T(4,128)} %bitcast.3) | data formatting | bytes 16384
  110.9 1.9 %copy.7 = f32[512,256]{1,0:T(8,128)} copy(f32[512,256]{1,0:T(8,128)} %get-tuple-element.8) | data formatting | bytes 1048576
